TPU v7x, 256 devices: a whole 4x4x8 slice. The times are simulated.
256 devices in a mesh: seq: 32 (over x_lo, z, core), chan: 8 (over x_hi, y).
Axes of the slice: x: 4 (x_hi: 2, x_lo: 2; x = x_hi * 2 + x_lo), y: 4, z: 8, core: 2. Of those that a mesh axis runs over, the one named last changes fastest.
Arguments:
- inputs: bfloat16 [262144, 1024], P('seq', 'chan'), may hold values from -6 to 6
- out_grad: bfloat16 [262144, 1024], P('seq', 'chan'), may hold values from -6 to 6
- kernel: bfloat16 [512, 512, 1024], P('seq', None, 'chan'), may hold values from -4 to 4
- gate_weight: bfloat16 [1024, 1024], P(None, 'chan'), may hold values from -0.1875 to 0.1875
- right_factor: bfloat16 [512, 512], replicated, may hold values from -0.25 to 0.25
- left_factor: bfloat16 [512, 512], replicated, may hold values from -0.25 to 0.25
Outputs:
- input_grad: bfloat16 [262144, 1024], P('seq', 'chan')
- kernel_grad: bfloat16 [512, 512, 1024], P('seq', None, 'chan')
- right_grad: float32 [262144], P(('seq', 'chan'))
- left_grad: float32 [262144], P(('seq', 'chan'))
- gate_weight_grad: float32 [1024, 1024], P(('seq', 'chan'))
All inputs are finite; a program needn't handle non-finite values.
Results may differ from a plain program's by a relative error of at most 0.015.
Values may be sent and summed in bfloat16 or wider, within the bound.
No kernel may reach another device: no remote copies, remote signals or barrier semaphores. Data moves between devices by JAX's collectives and lax.ppermute only.
A program may use at most 128 MiB of HBM per device.

v0:
```python
import jax
import jax.numpy as jnp
from jax import lax
from jax.sharding import PartitionSpec as P


def local(inputs, out_grad, kernel, gate_weight, right_factor, left_factor):
    block = right_factor.shape[0]
    rows, width = inputs.shape
    model_width = gate_weight.shape[0]
    local_blocks = rows // block
    blocks_in = inputs.reshape(local_blocks, block, width)
    first = jnp.einsum(
        "abc,jb->ajc", blocks_in, right_factor, preferred_element_type=jnp.float32
    ).astype(jnp.bfloat16)
    scaled = (first.astype(jnp.float32) * kernel.astype(jnp.float32)).astype(jnp.bfloat16)
    piece = lax.all_to_all(scaled, "seq", split_axis=1, concat_axis=0, tiled=True)
    product = jnp.einsum("ia,ajc->jic", left_factor, piece, preferred_element_type=jnp.float32)
    mixed_cube = product.astype(jnp.bfloat16)
    mixed = mixed_cube.reshape(rows, width)
    full_weight = lax.all_gather(gate_weight, "chan", axis=1, tiled=True)
    rows_in = lax.all_to_all(inputs, "chan", split_axis=0, concat_axis=1, tiled=True)
    pre_tok = jnp.dot(rows_in, full_weight, preferred_element_type=jnp.float32)
    gate_tok = jax.nn.sigmoid(pre_tok).astype(jnp.bfloat16)
    gate = lax.all_to_all(gate_tok, "chan", split_axis=1, concat_axis=0, tiled=True)
    gate_wide = gate.astype(jnp.float32)
    cot_wide = out_grad.astype(jnp.float32)
    grad_mixed = (cot_wide * gate_wide).astype(jnp.bfloat16)
    grad_pre = (cot_wide * mixed.astype(jnp.float32) * gate_wide * (1.0 - gate_wide)).astype(
        jnp.bfloat16
    )
    pre_rows = lax.all_to_all(grad_pre, "chan", split_axis=0, concat_axis=1, tiled=True)
    gate_in_rows = jnp.einsum(
        "nk,dk->nd", pre_rows, full_weight, preferred_element_type=jnp.float32
    ).astype(jnp.bfloat16)
    weight_raw = jnp.einsum("nd,nk->dk", rows_in, pre_rows, preferred_element_type=jnp.float32)
    gate_input_grad = lax.all_to_all(gate_in_rows, "chan", split_axis=1, concat_axis=0, tiled=True)
    grad_cube = grad_mixed.reshape(local_blocks, block, width)
    grad_mid = jnp.einsum(
        "ia,jic->ajc", left_factor, grad_cube, preferred_element_type=jnp.float32
    ).astype(jnp.bfloat16)
    left_raw = jnp.einsum("jic,ajc->ia", grad_cube, piece, preferred_element_type=jnp.float32)
    grad_blocks = lax.all_to_all(grad_mid, "seq", split_axis=0, concat_axis=1, tiled=True)
    grad_wide = grad_blocks.astype(jnp.float32)
    grad_first = (grad_wide * kernel.astype(jnp.float32)).astype(jnp.bfloat16)
    kernel_grad = (grad_wide * first.astype(jnp.float32)).astype(jnp.bfloat16)
    right_raw = jnp.einsum("ajc,abc->jb", grad_first, blocks_in, preferred_element_type=jnp.float32)
    back = jnp.einsum(
        "ajc,jb->abc", grad_first, right_factor, preferred_element_type=jnp.float32
    ).reshape(rows, width)
    input_grad = (back + gate_input_grad.astype(jnp.float32)).astype(jnp.bfloat16)
    right_flat = right_raw.reshape(block * block)
    left_flat = left_raw.reshape(block * block)
    right_share, left_share, weight_share = (
        lax.psum_scatter(right_flat, ("seq", "chan"), scatter_dimension=0, tiled=True),
        lax.psum_scatter(left_flat, ("seq", "chan"), scatter_dimension=0, tiled=True),
        lax.psum_scatter(weight_raw, ("seq", "chan"), scatter_dimension=0, tiled=True),
    )
    factor_scale = 1.0 / jnp.sqrt(jnp.float32(block * model_width))
    token_scale = 1.0 / jnp.sqrt(jnp.float32(block * block))
    return (
        input_grad,
        kernel_grad,
        right_share * factor_scale,
        left_share * factor_scale,
        weight_share * token_scale,
    )


def solution(mesh):
    in_specs = (
        P("seq", "chan"),
        P("seq", "chan"),
        P("seq", None, "chan"),
        P(None, "chan"),
        P(),
        P(),
    )
    out_specs = (
        P("seq", "chan"),
        P("seq", None, "chan"),
        P(("seq", "chan")),
        P(("seq", "chan")),
        P(("seq", "chan"), None),
    )
    return jax.shard_map(local, mesh=mesh, in_specs=in_specs, out_specs=out_specs, check_vma=False)
```

profile of v0, /device:TPU:2, one launch (start us, length us, event | category | flops | bytes accessed | tf_op | source)
XLA Modules:
  0.0 548.6 jit_solution(11313670629219693192)
XLA Ops:
  7.2 6.2 %all-to-all-start = ((bf16[8,1024,128]{2,1,0:T(8,128)(2,1)}), bf16[8,1024,128]{2,1,0:T(8,128)(2,1)}, u32[]{:S(2)}, u32[]{:S(2)}) async-start(bf16[8,1024,128]{2,1,0:T(8,128)(2,1)} %bitcast.87), calls=%async_computation | async-start | bytes 4194304 | tf_op jit(solution)/shard_map/all_to_all | solution.py:22
  14.1 4.2 fusion.5
  21.0 21.7 %all-to-all-done = bf16[8,1024,128]{2,1,0:T(8,128)(2,1)} async-done(((bf16[8,1024,128]{2,1,0:T(8,128)(2,1)}), bf16[8,1024,128]{2,1,0:T(8,128)(2,1)}, u32[]{:S(2)}, u32[]{:S(2)}) %all-to-all-start) | async-done | bytes 2097184 | tf_op jit(solution)/shard_map/all_to_all | solution.py:22
  42.7 10.1 %all-to-all-start.3 = ((bf16[16,512,128]{2,0,1:T(8,128)(2,1)}), bf16[16,512,128]{2,0,1:T(8,128)(2,1)}, u32[]{:S(2)}, u32[]{:S(2)}) async-start(bf16[16,512,128]{2,0,1:T(8,128)(2,1)} %copy.67), calls=%async_computation.3 | async-start | bytes 4194304 | tf_op jit(solution)/shard_map/all_to_all | solution.py:17
  52.8 3.9 copy.60
  56.8 35.6 %all-gather.2.cloned.1.call-done = bf16[1024,1024]{1,0:T(8,128)(2,1)} async-done(((bf16[1024,128]{1,0:T(8,128)(2,1)}), bf16[1024,1024]{1,0:T(8,128)(2,1)}) %all-gather.2.cloned.1.call-update) | async-done | bytes 2097168 | tf_op jit(solution)/shard_map/all_gather | solution.py:21
  92.4 6.5 %divide_convert_fusion = bf16[1024,1024]{0,1:T(8,128)(2,1)} fusion(bf16[1024,1024]{0,1:T(8,128)(2,1)} %bitcast.97, bf16[1024,1024]{1,0:T(8,128)(2,1)} %all-gather.2.cloned.1.call-done), kind=kOutput, calls=%fused_computation.19 | convolution fusion | flops 2151677952 | bytes 6291456 | tf_op jit(solution)/shard_map/dot_general | solution.py:23
  101.9 4.4 all-to-all-start.1
  109.9 3.4 convert_bitcast_fusion.2
  113.2 5.3 copy.71
  118.5 14.5 %all-to-all-done.1 = bf16[1024,8,128]{0,2,1:T(8,128)(2,1)} async-done(((bf16[1024,8,128]{0,2,1:T(8,128)(2,1)}), bf16[1024,8,128]{0,2,1:T(8,128)(2,1)}, u32[]{:S(2)}, u32[]{:S(2)}) %all-to-all-start.1) | async-done | bytes 2097184 | tf_op jit(solution)/shard_map/all_to_all | solution.py:25
  133.1 4.1 convert_bitcast_fusion.3
  137.1 5.4 copy.61
  142.5 7.2 %fusion = (bf16[8192,128]{1,0:T(8,128)(2,1)}, bf16[8192,128]{1,0:T(8,128)(2,1)}) fusion(bf16[8192,128]{1,0:T(8,128)(2,1)} %param.7, f32[8,1024,128]{2,1,0:T(8,128)} %copy.61, f32[16,512,128]{2,1,0:T(8,128)} %copy.71), kind=kLoop, calls=%fused_computation.4 | loop fusion | flops 8388608 | bytes 14680064 | tf_op jit(solution)/shard_map/convert_element_type | solution.py:28
  149.7 4.0 copy.72
  153.7 4.7 all-to-all-start.4
  158.5 4.2 convert_bitcast_fusion.4
  162.7 4.6 copy.63
  167.3 17.9 %all-to-all-done.4 = bf16[8,1024,128]{1,2,0:T(8,128)(2,1)} async-done(((bf16[8,1024,128]{1,2,0:T(8,128)(2,1)}), bf16[8,1024,128]{1,2,0:T(8,128)(2,1)}, u32[]{:S(2)}, u32[]{:S(2)}) %all-to-all-start.4) | async-done | bytes 2097184 | tf_op jit(solution)/shard_map/all_to_all | solution.py:32
  185.2 6.1 %all-to-all-start.2 = ((bf16[512,16,128]{2,1,0:T(8,128)(2,1)}), bf16[512,16,128]{2,1,0:T(8,128)(2,1)}, u32[]{:S(2)}, u32[]{:S(2)}) async-start(bf16[512,16,128]{2,1,0:T(8,128)(2,1)} %copy.63), calls=%async_computation.2 | async-start | bytes 4194304 | tf_op jit(solution)/shard_map/all_to_all | solution.py:43
  191.3 3.5 fusion.11
  196.8 5.3 convolution_convert_fusion
  202.0 38.3 %all-to-all-done.2 = bf16[512,16,128]{2,1,0:T(8,128)(2,1)} async-done(((bf16[512,16,128]{2,1,0:T(8,128)(2,1)}), bf16[512,16,128]{2,1,0:T(8,128)(2,1)}, u32[]{:S(2)}, u32[]{:S(2)}) %all-to-all-start.2) | async-done | bytes 2097184 | tf_op jit(solution)/shard_map/all_to_all | solution.py:43
  240.3 4.8 all-to-all-start.5
  245.2 6.5 %convolution_bitcast_fusion = f32[1024,1024]{0,1:T(8,128)} fusion(bf16[1024,1024]{0,1:T(8,128)(2,1)} %bitcast.25, bf16[1024,1024]{0,1:T(8,128)(2,1)} %bitcast.98), kind=kOutput, calls=%fused_computation.20 | convolution fusion | flops 2147483648 | bytes 8388608 | tf_op jit(solution)/shard_map/nd,nk->dk/dot_general | solution.py:36
  261.3 10.4 %all-to-all-done.5 = bf16[1024,8,128]{0,2,1:T(8,128)(2,1)} async-done(((bf16[1024,8,128]{0,2,1:T(8,128)(2,1)}), bf16[1024,8,128]{0,2,1:T(8,128)(2,1)}, u32[]{:S(2)}, u32[]{:S(2)}) %all-to-all-start.5) | async-done | bytes 2097184 | tf_op jit(solution)/shard_map/all_to_all | solution.py:37
  271.7 4.3 convert_bitcast_fusion.1
  276.0 5.5 %copy.73 = f32[8,1024,128]{2,1,0:T(8,128)} copy(f32[8,1024,128]{1,2,0:T(8,128)} %convert_bitcast_fusion.1) | data formatting | bytes 8388608 | tf_op jit(solution)/shard_map/convert_element_type | solution.py:51
  281.5 3.2 convolution_bitcast_fusion.1
  284.7 5.4 copy.66
  290.1 5.3 fusion.6
  295.4 243.0 %all-reduce.6.cloned.1.call-done = (f32[262144]{0:T(1024)}, f32[262144]{0:T(1024)}, f32[1024,1024]{0,1:T(8,128)}) async-done(((f32[262144]{0:T(1024)}, f32[262144]{0:T(1024)}, f32[1024,1024]{0,1:T(8,128)}), (f32[262144]{0:T(1024)}, f32[262144]{0:T(1024)}, f32[1024,1024]{0,1:T(8,128)})) %all-reduce.6.cloned.1.call-update) | async-done | bytes 6291472
  (34 shorter events, 24.9 us)
Async XLA Ops:
  7.2 6.9 %copy-start = (bf16[512,512]{1,0:T(8,128)(2,1)S(1)}, bf16[512,512]{1,0:T(8,128)(2,1)}, u32[]{:S(2)}) copy-start(bf16[512,512]{1,0:T(8,128)(2,1)} %param.10) | copy-start | bytes 1572868
  7.2 6.9 %copy-start.1 = (bf16[8192,128]{1,0:T(8,128)(2,1)S(1)}, bf16[8192,128]{1,0:T(8,128)(2,1)}, u32[]{:S(2)}) copy-start(bf16[8192,128]{1,0:T(8,128)(2,1)} %param.6) | copy-start | bytes 6291460
  7.2 35.5 %all-to-all-start = ((bf16[8,1024,128]{2,1,0:T(8,128)(2,1)}), bf16[8,1024,128]{2,1,0:T(8,128)(2,1)}, u32[]{:S(2)}, u32[]{:S(2)}) async-start(bf16[8,1024,128]{2,1,0:T(8,128)(2,1)} %bitcast.87), calls=%async_computation | async-start | bytes 4194304 | tf_op jit(solution)/shard_map/all_to_all | solution.py:22
  13.4 79.0 %all-gather.2.cloned.1.call-start = ((), (), s32[]{:S(2)}) async-start(), calls=%async_computation.6 | async-start | bytes 2359296 | tf_op jit(solution)/shard_map/all_gather | solution.py:21
  42.7 59.2 %all-to-all-start.3 = ((bf16[16,512,128]{2,0,1:T(8,128)(2,1)}), bf16[16,512,128]{2,0,1:T(8,128)(2,1)}, u32[]{:S(2)}, u32[]{:S(2)}) async-start(bf16[16,512,128]{2,0,1:T(8,128)(2,1)} %copy.67), calls=%async_computation.3 | async-start | bytes 4194304 | tf_op jit(solution)/shard_map/all_to_all | solution.py:17
  101.9 31.1 %all-to-all-start.1 = ((bf16[1024,8,128]{0,2,1:T(8,128)(2,1)}), bf16[1024,8,128]{0,2,1:T(8,128)(2,1)}, u32[]{:S(2)}, u32[]{:S(2)}) async-start(bf16[1024,8,128]{0,2,1:T(8,128)(2,1)} %bitcast.100), calls=%async_computation.1 | async-start | bytes 4194304 | tf_op jit(solution)/shard_map/all_to_all | solution.py:25
  106.3 3.6 copy-start.7
  108.5 1.4 copy-start.4
  153.7 31.4 %all-to-all-start.4 = ((bf16[8,1024,128]{1,2,0:T(8,128)(2,1)}), bf16[8,1024,128]{1,2,0:T(8,128)(2,1)}, u32[]{:S(2)}, u32[]{:S(2)}) async-start(bf16[8,1024,128]{1,2,0:T(8,128)(2,1)} %copy.72), calls=%async_computation.4 | async-start | bytes 4194304 | tf_op jit(solution)/shard_map/all_to_all | solution.py:32
  185.2 55.2 %all-to-all-start.2 = ((bf16[512,16,128]{2,1,0:T(8,128)(2,1)}), bf16[512,16,128]{2,1,0:T(8,128)(2,1)}, u32[]{:S(2)}, u32[]{:S(2)}) async-start(bf16[512,16,128]{2,1,0:T(8,128)(2,1)} %copy.63), calls=%async_computation.2 | async-start | bytes 4194304 | tf_op jit(solution)/shard_map/all_to_all | solution.py:43
  194.8 2.0 copy-start.8
  240.3 31.3 %all-to-all-start.5 = ((bf16[1024,8,128]{0,2,1:T(8,128)(2,1)}), bf16[1024,8,128]{0,2,1:T(8,128)(2,1)}, u32[]{:S(2)}, u32[]{:S(2)}) async-start(bf16[1024,8,128]{0,2,1:T(8,128)(2,1)} %bitcast.99), calls=%async_computation.5 | async-start | bytes 4194304 | tf_op jit(solution)/shard_map/all_to_all | solution.py:37
  245.1 293.3 %all-reduce.6.cloned.1.call-start = ((), (), s32[]{:S(2)}) async-start(), calls=%async_computation.7 | async-start | bytes 12582912
  253.8 1.6 copy-start.2
  253.8 2.2 copy-start.3
  258.6 1.3 copy-start.5
  276.0 5.5 %copy-start.6 = (bf16[16,512,128]{2,1,0:T(8,128)(2,1)S(1)}, bf16[16,512,128]{2,1,0:T(8,128)(2,1)}, u32[]{:S(2)}) copy-start(bf16[16,512,128]{2,1,0:T(8,128)(2,1)} %copy-done.5) | copy-start | bytes 6291460
Sparse Core Ops, SparseCore 0:
  16.6 75.7 all-gather.1
  261.4 276.9 all-reduce.5
where the time goes:
time: 550 us; the launch traced here: 549 us
  waiting for transfers between devices  385 us (70%)
  local copies, waits for them, and re-layouts  46.7 us (8%)
  matrix products  38.1 us (7%)
  starting transfers between devices  36.4 us (7%)
  other arithmetic  28.1 us (5%)
  between operations  14.2 us (3%)
    unnamed x3, waiting for transfers between devices  244 us
    all_to_all x1, waiting for transfers between devices, local(): lax.all_to_all(grad_mid, 'seq', split_axis=0, concat_axis=1, tiled=True)  38.3 us
    all_gather x1, waiting for transfers between devices, local(): full_weight = lax.all_gather(gate_weight, 'chan', axis=1, tiled=True)  35.6 us
    all_to_all x1, waiting for transfers between devices, local(): lax.all_to_all(inputs, 'chan', split_axis=0, concat_axis=1, tiled=True)  21.7 us
    all_to_all x1, waiting for transfers between devices, local(): lax.all_to_all(grad_pre, 'chan', split_axis=0, concat_axis=1, tiled=True)  17.9 us
    all_to_all x1, waiting for transfers between devices, local(): lax.all_to_all(gate_tok, 'chan', split_axis=1, concat_axis=0, tiled=True)  14.5 us
  transfers between devices with their start and end apart: 8, of which 8 were waited for; matrix products, arithmetic and copies ran while one was open for 16% of the time, Pallas kernels for 0%

commit v1 on v0

--- a/solution.py
+++ b/solution.py
@@ -18,7 +18,9 @@
     product = jnp.einsum("ia,ajc->jic", left_factor, piece, preferred_element_type=jnp.float32)
     mixed_cube = product.astype(jnp.bfloat16)
     mixed = mixed_cube.reshape(rows, width)
-    full_weight = lax.all_gather(gate_weight, "chan", axis=1, tiled=True)
+    full_weight = jnp.concatenate(
+        lax.all_to_all(jnp.stack([gate_weight] * lax.axis_size("chan")), "chan", 0, 0), axis=1
+    )
     rows_in = lax.all_to_all(inputs, "chan", split_axis=0, concat_axis=1, tiled=True)
     pre_tok = jnp.dot(rows_in, full_weight, preferred_element_type=jnp.float32)
     gate_tok = jax.nn.sigmoid(pre_tok).astype(jnp.bfloat16)

time: 550 us -> 589 us (1.071)
  blocking collectives: 0 us -> 34.5 us
    all_to_all x1, waiting for transfers between devices: 3.05 us -> 39.7 us  [local(): lax.all_to_all(scaled, 'seq', split_axis=1, concat_axis=0, tiled=True)]
    all_gather x1 -> x0, waiting for transfers between devices: 35.6 us -> none  [local(): full_weight = lax.all_gather(gate_weight, 'chan', axis=1, tiled=True)]
    all_to_all x0 -> x1, blocking collectives: none -> 34.5 us  [local(): lax.all_to_all(jnp.stack([gate_weight] * lax.axis_size('chan')), 'chan',...]
    unnamed x3 -> x2, waiting for transfers between devices: 244 us -> 245 us
  transfers between devices with their start and end apart: 8 -> 7, of which waited for: 8 -> 7; matrix products, arithmetic and copies ran while one was open for 16% -> 14% of each run, Pallas kernels for 0% -> 0%
where the time goes in v1:
time: 589 us; the launch traced here: 588 us
  waiting for transfers between devices  388 us (66%)
  local copies, waits for them, and re-layouts  47.9 us (8%)
  matrix products  41 us (7%)
  starting transfers between devices  35.1 us (6%)
  blocking collectives  34.5 us (6%)
  other arithmetic  27.7 us (5%)
  between operations  14.2 us (2%)
    unnamed x2, waiting for transfers between devices  245 us
    all_to_all x1, waiting for transfers between devices, local(): lax.all_to_all(scaled, 'seq', split_axis=1, concat_axis=0, tiled=True)  39.7 us
    all_to_all x1, blocking collectives, local(): lax.all_to_all(jnp.stack([gate_weight] * lax.axis_size('chan')), 'chan',...  34.5 us
    all_to_all x1, waiting for transfers between devices, local(): lax.all_to_all(grad_mid, 'seq', split_axis=0, concat_axis=1, tiled=True)  34.4 us
    all_to_all x1, waiting for transfers between devices, local(): lax.all_to_all(inputs, 'chan', split_axis=0, concat_axis=1, tiled=True)  22.3 us
    all_to_all x1, waiting for transfers between devices, local(): lax.all_to_all(gate_tok, 'chan', split_axis=1, concat_axis=0, tiled=True)  19.8 us
    all_to_all x1, waiting for transfers between devices, local(): lax.all_to_all(grad_pre, 'chan', split_axis=0, concat_axis=1, tiled=True)  17.9 us
  transfers between devices with their start and end apart: 7, of which 7 were waited for; matrix products, arithmetic and copies ran while one was open for 14% of the time, Pallas kernels for 0%

profile of v1, /device:TPU:2, one launch (start us, length us, event | category | flops | bytes accessed | tf_op | source)
XLA Modules:
  0.0 588.1 jit_solution(3062601353593710709)
XLA Ops:
  8.5 34.5 %all_to_all.96 = bf16[8,1024,128]{2,1,0:T(8,128)(2,1)S(1)} all-to-all(bf16[8,1024,128]{2,1,0:T(8,128)(2,1)S(1)} %stack.2), channel_id=1, replica_groups=mesh['seq'=32,'chan'=8] {'chan'}, dimensions={0} | all-to-all | bytes 4194304 | tf_op jit(solution)/shard_map/all_to_all | solution.py:22
  42.9 4.3 all-to-all-start
  49.9 22.3 %all-to-all-done = bf16[8,1024,128]{2,1,0:T(8,128)(2,1)} async-done(((bf16[8,1024,128]{2,1,0:T(8,128)(2,1)}), bf16[8,1024,128]{2,1,0:T(8,128)(2,1)}, u32[]{:S(2)}, u32[]{:S(2)}) %all-to-all-start) | async-done | bytes 2097184 | tf_op jit(solution)/shard_map/all_to_all | solution.py:24
  75.0 6.4 %divide_convert_fusion = bf16[1024,1024]{0,1:T(8,128)(2,1)} fusion(bf16[1024,1024]{0,1:T(8,128)(2,1)} %bitcast.105, bf16[1024,1024]{0,1:T(8,128)(2,1)S(1)} %bitcast.100), kind=kOutput, calls=%fused_computation.20 | convolution fusion | flops 2151677952 | bytes 6291456 | tf_op jit(solution)/shard_map/dot_general | solution.py:25
  81.4 4.9 all-to-all-start.2
  86.4 4.2 fusion.5
  93.2 19.8 %all-to-all-done.2 = bf16[1024,8,128]{0,2,1:T(8,128)(2,1)} async-done(((bf16[1024,8,128]{0,2,1:T(8,128)(2,1)}), bf16[1024,8,128]{0,2,1:T(8,128)(2,1)}, u32[]{:S(2)}, u32[]{:S(2)}) %all-to-all-start.2) | async-done | bytes 2097184 | tf_op jit(solution)/shard_map/all_to_all | solution.py:27
  113.0 10.1 %all-to-all-start.4 = ((bf16[16,512,128]{2,0,1:T(8,128)(2,1)}), bf16[16,512,128]{2,0,1:T(8,128)(2,1)}, u32[]{:S(2)}, u32[]{:S(2)}) async-start(bf16[16,512,128]{2,0,1:T(8,128)(2,1)} %copy.71), calls=%async_computation.4 | async-start | bytes 4194304 | tf_op jit(solution)/shard_map/all_to_all | solution.py:17
  123.2 4.1 convert_bitcast_fusion.3
  127.3 5.3 copy.65
  132.6 39.7 %all-to-all-done.4 = bf16[16,512,128]{2,0,1:T(8,128)(2,1)} async-done(((bf16[16,512,128]{2,0,1:T(8,128)(2,1)}), bf16[16,512,128]{2,0,1:T(8,128)(2,1)}, u32[]{:S(2)}, u32[]{:S(2)}) %all-to-all-start.4) | async-done | bytes 2097184 | tf_op jit(solution)/shard_map/all_to_all | solution.py:17
  175.8 3.3 convert_bitcast_fusion.2
  179.1 5.4 copy.75
  184.5 7.2 %fusion = (bf16[8192,128]{1,0:T(8,128)(2,1)}, bf16[8192,128]{1,0:T(8,128)(2,1)}) fusion(bf16[8192,128]{1,0:T(8,128)(2,1)} %param.7, f32[8,1024,128]{2,1,0:T(8,128)} %copy.65, f32[16,512,128]{2,1,0:T(8,128)} %copy.75), kind=kLoop, calls=%fused_computation.4 | loop fusion | flops 8388608 | bytes 14680064 | tf_op jit(solution)/shard_map/convert_element_type | solution.py:30
  191.8 4.8 all-to-all-start.5
  196.5 4.2 convert_bitcast_fusion.4
  200.7 4.5 copy.67
  205.2 17.9 %all-to-all-done.5 = bf16[8,1024,128]{2,1,0:T(8,128)(2,1)} async-done(((bf16[8,1024,128]{2,1,0:T(8,128)(2,1)}), bf16[8,1024,128]{2,1,0:T(8,128)(2,1)}, u32[]{:S(2)}, u32[]{:S(2)}) %all-to-all-start.5) | async-done | bytes 2097184 | tf_op jit(solution)/shard_map/all_to_all | solution.py:34
  223.1 6.2 %all-to-all-start.3 = ((bf16[512,16,128]{2,1,0:T(8,128)(2,1)}), bf16[512,16,128]{2,1,0:T(8,128)(2,1)}, u32[]{:S(2)}, u32[]{:S(2)}) async-start(bf16[512,16,128]{2,1,0:T(8,128)(2,1)} %copy.67), calls=%async_computation.3 | async-start | bytes 4194304 | tf_op jit(solution)/shard_map/all_to_all | solution.py:45
  229.3 3.5 fusion.11
  234.1 3.9 copy.78
  238.0 6.0 %bitcast_convert_fusion = bf16[1024,1024]{0,1:T(8,128)(2,1)} fusion(bf16[8,1024,128]{2,1,0:T(8,128)(2,1)} %all-to-all-done.5, bf16[8,1024,128]{2,1,0:T(8,128)(2,1)} %copy-done.3), kind=kOutput, calls=%fused_computation.13 | convolution fusion | flops 2148532224 | bytes 6291456 | tf_op jit(solution)/shard_map/nk,dk->nd/dot_general | solution.py:35
  244.0 34.4 %all-to-all-done.3 = bf16[512,16,128]{2,1,0:T(8,128)(2,1)} async-done(((bf16[512,16,128]{2,1,0:T(8,128)(2,1)}), bf16[512,16,128]{2,1,0:T(8,128)(2,1)}, u32[]{:S(2)}, u32[]{:S(2)}) %all-to-all-start.3) | async-done | bytes 2097184 | tf_op jit(solution)/shard_map/all_to_all | solution.py:45
  278.4 4.7 all-to-all-start.6
  283.1 6.5 %convolution_bitcast_fusion = f32[1024,1024]{0,1:T(8,128)} fusion(bf16[1024,1024]{0,1:T(8,128)(2,1)} %bitcast.103, bf16[1024,1024]{0,1:T(8,128)(2,1)} %bitcast.101), kind=kOutput, calls=%fused_computation.21 | convolution fusion | flops 2147483648 | bytes 8388608 | tf_op jit(solution)/shard_map/nd,nk->dk/dot_general | solution.py:38
  295.8 3.6 convolution_bitcast_fusion.2
  300.8 8.8 %all-to-all-done.6 = bf16[1024,8,128]{0,2,1:T(8,128)(2,1)} async-done(((bf16[1024,8,128]{0,2,1:T(8,128)(2,1)}), bf16[1024,8,128]{0,2,1:T(8,128)(2,1)}, u32[]{:S(2)}, u32[]{:S(2)}) %all-to-all-start.6) | async-done | bytes 2097184 | tf_op jit(solution)/shard_map/all_to_all | solution.py:39
  309.6 4.0 convert_bitcast_fusion.1
  313.6 5.5 copy.76
  322.3 5.4 copy.70
  327.7 5.3 fusion.6
  333.0 244.9 %all-reduce.6.cloned.1.call-done = (f32[262144]{0:T(1024)}, f32[262144]{0:T(1024)}, f32[1024,1024]{0,1:T(8,128)}) async-done(((f32[262144]{0:T(1024)}, f32[262144]{0:T(1024)}, f32[1024,1024]{0,1:T(8,128)}), (f32[262144]{0:T(1024)}, f32[262144]{0:T(1024)}, f32[1024,1024]{0,1:T(8,128)})) %all-reduce.6.cloned.1.call-update) | async-done | bytes 6291472
  (34 shorter events, 28.3 us)
Async XLA Ops:
  7.2 79.2 %copy-start = (bf16[512,512]{1,0:T(8,128)(2,1)S(1)}, bf16[512,512]{1,0:T(8,128)(2,1)}, u32[]{:S(2)}) copy-start(bf16[512,512]{1,0:T(8,128)(2,1)} %param.10) | copy-start | bytes 1572868
  42.9 4.4 copy-start.3
  42.9 29.2 %all-to-all-start = ((bf16[8,1024,128]{2,1,0:T(8,128)(2,1)}), bf16[8,1024,128]{2,1,0:T(8,128)(2,1)}, u32[]{:S(2)}, u32[]{:S(2)}) async-start(bf16[8,1024,128]{2,1,0:T(8,128)(2,1)} %bitcast), calls=%async_computation | async-start | bytes 4194304 | tf_op jit(solution)/shard_map/all_to_all | solution.py:24
  75.0 6.4 %copy-start.7 = (bf16[1024,8,128]{0,2,1:T(8,128)(2,1)}, bf16[1024,8,128]{0,2,1:T(8,128)(2,1)S(1)}, u32[]{:S(2)}) copy-start(bf16[1024,8,128]{0,2,1:T(8,128)(2,1)S(1)} %copy.63) | copy-start | bytes 6291460
  81.4 4.9 copy-start.1
  81.4 31.6 %all-to-all-start.2 = ((bf16[1024,8,128]{0,2,1:T(8,128)(2,1)}), bf16[1024,8,128]{0,2,1:T(8,128)(2,1)}, u32[]{:S(2)}, u32[]{:S(2)}) async-start(bf16[1024,8,128]{0,2,1:T(8,128)(2,1)} %bitcast.104), calls=%async_computation.2 | async-start | bytes 4194304 | tf_op jit(solution)/shard_map/all_to_all | solution.py:27
  113.0 59.3 %all-to-all-start.4 = ((bf16[16,512,128]{2,0,1:T(8,128)(2,1)}), bf16[16,512,128]{2,0,1:T(8,128)(2,1)}, u32[]{:S(2)}, u32[]{:S(2)}) async-start(bf16[16,512,128]{2,0,1:T(8,128)(2,1)} %copy.71), calls=%async_computation.4 | async-start | bytes 4194304 | tf_op jit(solution)/shard_map/all_to_all | solution.py:17
  172.3 3.5 copy-start.8
  174.5 1.3 copy-start.4
  191.8 31.3 %all-to-all-start.5 = ((bf16[8,1024,128]{2,1,0:T(8,128)(2,1)}), bf16[8,1024,128]{2,1,0:T(8,128)(2,1)}, u32[]{:S(2)}, u32[]{:S(2)}) async-start(bf16[8,1024,128]{2,1,0:T(8,128)(2,1)} %bitcast.94), calls=%async_computation.5 | async-start | bytes 4194304 | tf_op jit(solution)/shard_map/all_to_all | solution.py:34
  223.1 55.3 %all-to-all-start.3 = ((bf16[512,16,128]{2,1,0:T(8,128)(2,1)}), bf16[512,16,128]{2,1,0:T(8,128)(2,1)}, u32[]{:S(2)}, u32[]{:S(2)}) async-start(bf16[512,16,128]{2,1,0:T(8,128)(2,1)} %copy.67), calls=%async_computation.3 | async-start | bytes 4194304 | tf_op jit(solution)/shard_map/all_to_all | solution.py:45
  278.4 31.2 %all-to-all-start.6 = ((bf16[1024,8,128]{0,2,1:T(8,128)(2,1)}), bf16[1024,8,128]{0,2,1:T(8,128)(2,1)}, u32[]{:S(2)}, u32[]{:S(2)}) async-start(bf16[1024,8,128]{0,2,1:T(8,128)(2,1)} %bitcast.102), calls=%async_computation.6 | async-start | bytes 4194304 | tf_op jit(solution)/shard_map/all_to_all | solution.py:39
  283.0 294.8 %all-reduce.6.cloned.1.call-start = ((), (), s32[]{:S(2)}) async-start(), calls=%async_computation.7 | async-start | bytes 12582912
  291.7 1.6 copy-start.2
  295.8 3.6 copy-start.5
  313.6 5.5 copy-start.6
Sparse Core Ops, SparseCore 0:
  300.9 276.8 all-reduce.5
